TPU v7x, 32 devices: a whole 2x2x4 slice. The times are simulated.
32 devices in a mesh: ifg: 8 (over z, core), strip: 4 (over y, x).
Axes of the slice: x: 2, y: 2, z: 4, core: 2. Of those that a mesh axis runs over, the one named last changes fastest.
Arguments:
- grad_x: float32 [64, 256, 1024], P('ifg', 'strip'), may hold values from -3 to 3
- grad_y: float32 [64, 256, 1024], P('ifg', 'strip'), may hold values from -3 to 3
- coherence: float32 [64, 256, 1024], P('ifg', 'strip'), may hold values from 0 to 1, as said below
- pairs: int32 [64, 2], replicated, may hold values from 0 to 31, as said below
Outputs:
- unwrapped: float32 [64, 256, 1024], P('ifg', 'strip')
- series: float32 [32, 256, 1024], P('ifg', 'strip')
Inputs may be any that keep to these rules, and one draw needn't show every extreme that they name: Every row names an earlier date first and a later date second; the pairs connect all 32 dates. `coherence`: positive weights.
All inputs are finite; a program needn't handle non-finite values.
Results may differ from a plain program's by a relative error of at most 0.0003.
Values sent between devices are 32-bit elements; how exact they have to be, the bound alone decides.
No kernel may reach another device: no remote copies, remote signals or barrier semaphores. Data moves between devices by JAX's collectives and lax.ppermute only.
A program may use at most 64 MiB of HBM per device.

v0:
```python
import jax
import jax.numpy as jnp
from jax import lax
from jax.sharding import PartitionSpec as P

DATES = 32
ITERS = 3
damping = 0.1


def extended(x, sides, width):
    for axis, dim in sides:
        size, length = (lax.axis_size(axis), x.shape[dim])
        up = [(i, (i + 1) % size) for i in range(size - 1)]
        down = [(j, i) for i, j in up]
        last = lax.slice_in_dim(x, length - width, length, axis=dim)
        initial = lax.slice_in_dim(x, 0, width, axis=dim)
        before = lax.ppermute(last, axis, up)
        after = lax.ppermute(initial, axis, down)
        x = jnp.concatenate([before, x, after], axis=dim)
    return x


def prev_col(field):
    return jnp.pad(field, ((0, 0), (0, 0), (1, 0)))[:, :, :-1]


def inverse_map(pairs):
    slots = jnp.arange(DATES, dtype=jnp.int32)
    design = (pairs[:, 1:2] == slots[None, :]).astype(jnp.float32) - (
        pairs[:, 0:1] == slots[None, :]
    ).astype(jnp.float32)
    normal = jnp.dot(design.T, design, precision=lax.Precision.HIGHEST) + 1.0
    factor = jnp.linalg.cholesky(normal)
    return jax.scipy.linalg.cho_solve((factor, True), design.T)


def operate(field, wx, wy_ext):
    padded = extended(field, (("strip", 1),), 1)
    diff_y = padded[:, 1:, :] - padded[:, :-1, :]
    flux_y = wy_ext * diff_y
    diff_x = jnp.pad(field[:, :, 1:] - field[:, :, :-1], ((0, 0), (0, 0), (0, 1)))
    flux_x = wx * diff_x
    return damping * field - (flux_x - prev_col(flux_x) + flux_y[:, 1:, :] - flux_y[:, :-1, :])


def two_products(residual, image):
    return lax.psum(
        (jnp.sum(residual * residual, axis=(1, 2)), jnp.sum(residual * image, axis=(1, 2))), "strip"
    )


def on_device(grad_x, grad_y, coherence, pairs):
    stacked = jnp.stack([coherence, grad_y])
    padded = extended(stacked, (("strip", 2),), 1)
    weight_ext = padded[0]
    grad_y_ext = padded[1]
    wy_ext = weight_ext[:, :-1, :] * weight_ext[:, 1:, :]
    flux_y = wy_ext * grad_y_ext[:, :-1, :]
    wx = jnp.pad(coherence[:, :, :-1] * coherence[:, :, 1:], ((0, 0), (0, 0), (0, 1)))
    flux_x = wx * grad_x
    rhs = -(flux_x - prev_col(flux_x) + flux_y[:, 1:, :] - flux_y[:, :-1, :])

    def apply_op(field):
        return operate(field, wx, wy_ext)

    solution = jnp.zeros_like(rhs)
    residual = rhs
    image = apply_op(residual)
    norm_now, product = two_products(residual, image)
    alpha = norm_now / product
    direction, along = (residual, image)
    for step in range(ITERS):
        solution = solution + alpha[:, None, None] * direction
        residual = residual - alpha[:, None, None] * along
        if step + 1 < ITERS:
            image = apply_op(residual)
            norm_next, product = two_products(residual, image)
            ratio = norm_next / norm_now
            alpha = norm_next / (product - ratio * norm_next / alpha)
            direction = residual + ratio[:, None, None] * direction
            along = image + ratio[:, None, None] * along
            norm_now = norm_next
    mapping = inverse_map(pairs)
    local = jnp.einsum(
        "dk,krc->drc",
        mapping,
        lax.all_to_all(solution, "ifg", split_axis=2, concat_axis=0, tiled=True),
        precision=lax.Precision.HIGHEST,
    )
    series = lax.all_to_all(local, "ifg", split_axis=0, concat_axis=2, tiled=True)
    return (solution, series)


def solution(mesh):
    in_specs = (P("ifg", "strip", None), P("ifg", "strip", None), P("ifg", "strip", None), P())
    out_specs = (P("ifg", "strip", None), P("ifg", "strip", None))
    return jax.shard_map(
        on_device, mesh=mesh, in_specs=in_specs, out_specs=out_specs, check_vma=False
    )
```

profile of v0, /device:TPU:0, one launch (start us, length us, event | category | flops | bytes accessed | tf_op | source)
XLA Modules:
  0.0 210.9 jit_solution(3839215137288973112)
XLA Ops:
  0.6 3.0 %copy.42 = f32[8,64,1024]{2,0,1:T(8,128)S(1)} copy(f32[8,64,1024]{2,1,0:T(8,128)} %param.6) | data formatting | bytes 4194304 | tf_op args[2]
  4.9 4.9 %collective-permute-start = (f32[2,8,1,1024]{3,1,2,0:T(8,128)S(1)}, f32[2,8,1,1024]{3,1,2,0:T(8,128)S(1)}, u32[]{:S(2)}, u32[]{:S(2)}) collective-permute-start(f32[2,8,1,1024]{3,1,2,0:T(8,128)S(1)} %get-tuple-element.30), channel_id=1, source_target_pairs={{0,1},{1,2},{2,3},{4,5},{5,6},{6,7},{8,9},{9,10},{10,11},{12,13},{... | collective-permute-start | bytes 196616 | tf_op jit(solution)/shard_map/ppermute | solution.py:18
  9.7 1.4 collective-permute-start.1
  11.8 1.4 copy_multiply_fusion
  13.2 2.9 %collective-permute-done.1 = f32[2,8,1,1024]{3,1,2,0:T(8,128)S(1)} collective-permute-done((f32[2,8,1,1024]{3,1,2,0:T(8,128)S(1)}, f32[2,8,1,1024]{3,1,2,0:T(8,128)S(1)}, u32[]{:S(2)}, u32[]{:S(2)}) %collective-permute-start.1) | collective-permute-done | bytes 65568 | tf_op jit(solution)/shard_map/ppermute | solution.py:19
  19.0 1.3 collective-permute-start.2
  20.3 4.9 %collective-permute-start.3 = (f32[8,1,1024]{2,0,1:T(8,128)S(1)}, f32[8,1,1024]{2,0,1:T(8,128)S(1)}, u32[]{:S(2)}, u32[]{:S(2)}) collective-permute-start(f32[8,1,1024]{2,0,1:T(8,128)S(1)} %get-tuple-element.36), channel_id=1, source_target_pairs={{0,1},{1,2},{2,3},{4,5},{5,6},{6,7},{8,9},{9,10},{10,11},{12,13},{... | collective-permute-start | bytes 98312 | tf_op jit(solution)/shard_map/ppermute | solution.py:18
  27.5 2.5 %multiply_reduce_fusion.3 = (f32[8]{0:T(128)S(1)}, f32[8]{0:T(128)S(1)}, f32[8,64,1024]{2,0,1:T(8,128)}) fusion(f32[8,64,1024]{2,0,1:T(8,128)S(1)} %get-tuple-element.25, f32[8,65,1024]{2,0,1:T(8,128)S(1)} %fusion, f32[8,64,1024]{2,0,1:T(8,128)S(1)} %pad_multiply_fusion.2), kind=kLoop, calls=%fused_computation.48 | loop fusion | flops 5242864 | bytes 10485824 | tf_op jit(solution)/shard_map/reduce_sum | solution.py:49
  30.0 10.7 %all-reduce.10 = (f32[8]{0:T(128)S(1)}, f32[8]{0:T(128)S(1)}) all-reduce(f32[8]{0:T(128)S(1)} %get-tuple-element.11, f32[8]{0:T(128)S(1)} %get-tuple-element.10), channel_id=1, replica_groups=mesh['ifg'=8,'strip'=4] {'strip'}, use_global_device_ids=true, to_apply=%region_1.2 | all-reduce | flops 16 | bytes 128 | tf_op jit(solution)/shard_map/psum | solution.py:48
  40.7 2.7 %multiply_subtract_fusion.1 = f32[8,64,1024]{2,0,1:T(8,128)S(1)} fusion(f32[8,64,1024]{2,0,1:T(8,128)} %get-tuple-element.23, f32[8]{0:T(128)S(1)} %div.29, f32[8,64,1024]{2,0,1:T(8,128)} %copy-done.8), kind=kLoop, calls=%fused_computation.47 | loop fusion | flops 1572864 | bytes 6291488 | tf_op jit(solution)/shard_map/sub | solution.py:75
  44.1 1.3 collective-permute-start.4
  45.4 4.9 %collective-permute-start.5 = (f32[8,1,1024]{2,0,1:T(8,128)S(1)}, f32[8,1,1024]{2,0,1:T(8,128)S(1)}, u32[]{:S(2)}, u32[]{:S(2)}) collective-permute-start(f32[8,1,1024]{2,0,1:T(8,128)S(1)} %get-tuple-element.34), channel_id=1, source_target_pairs={{0,1},{1,2},{2,3},{4,5},{5,6},{6,7},{8,9},{9,10},{10,11},{12,13},{... | collective-permute-start | bytes 98312 | tf_op jit(solution)/shard_map/ppermute | solution.py:18
  53.4 10.6 %all-reduce.9 = (f32[8]{0:T(128)S(1)}, f32[8]{0:T(128)S(1)}) all-reduce(f32[8]{0:T(128)S(1)} %get-tuple-element.9, f32[8]{0:T(128)S(1)} %get-tuple-element.8), channel_id=1, replica_groups=mesh['ifg'=8,'strip'=4] {'strip'}, use_global_device_ids=true, to_apply=%region_5.6 | all-reduce | flops 16 | bytes 128 | tf_op jit(solution)/shard_map/psum | solution.py:48
  64.1 5.8 %multiply_subtract_fusion = f32[8,64,1024]{2,0,1:T(8,128)S(1)} fusion(f32[8,64,1024]{2,0,1:T(8,128)S(1)} %multiply_subtract_fusion.1, f32[8,64,1024]{2,0,1:T(8,128)} %get-tuple-element.23, f32[8]{0:T(128)S(1)} %get-tuple-element.22, f32[8]{0:T(128)S(1)} %get-tuple-element.20, f32[8,65,1024]{2,0,1:T(8,128)} %copy-done.4, f32[8,64,1024]{2,0,1:T(8,128)} %copy-done.9), kind=kLoop, calls=%fused_computation.43 | loop fusion | flops 4718592 | bytes 12582976 | tf_op jit(solution)/shard_map/sub | solution.py:75
  70.6 1.4 collective-permute-start.6
  72.0 4.7 %collective-permute-start.7 = (f32[8,1,1024]{2,0,1:T(8,128)S(1)}, f32[8,1,1024]{2,0,1:T(8,128)S(1)}, u32[]{:S(2)}, u32[]{:S(2)}) collective-permute-start(f32[8,1,1024]{2,0,1:T(8,128)S(1)} %get-tuple-element.32), channel_id=1, source_target_pairs={{0,1},{1,2},{2,3},{4,5},{5,6},{6,7},{8,9},{9,10},{10,11},{12,13},{... | collective-permute-start | bytes 98312 | tf_op jit(solution)/shard_map/ppermute | solution.py:18
  79.9 10.7 %all-reduce.8 = (f32[8]{0:T(128)S(1)}, f32[8]{0:T(128)S(1)}) all-reduce(f32[8]{0:T(128)S(1)} %get-tuple-element.7, f32[8]{0:T(128)S(1)} %get-tuple-element.6), channel_id=1, replica_groups=mesh['ifg'=8,'strip'=4] {'strip'}, use_global_device_ids=true, to_apply=%region_9.10 | all-reduce | flops 16 | bytes 128 | tf_op jit(solution)/shard_map/psum | solution.py:48
  90.6 4.4 %multiply_add_fusion = f32[8,64,1024]{2,0,1:T(8,128)} fusion(f32[8,64,1024]{2,0,1:T(8,128)} %copy-done, f32[8,64,1024]{2,0,1:T(8,128)S(1)} %multiply_subtract_fusion.1, f32[8]{0:T(128)S(1)} %get-tuple-element.19, f32[8]{0:T(128)S(1)} %get-tuple-element.18, f32[8]{0:T(128)S(1)} %get-tuple-element.22, f32[8]{0:T(128)S(1)} %get-tuple-element.20, f32[8]{0:T(128)S(1)} %div.29, ...), kind=kLoop, calls=%fused_computation.40 | loop fusion | flops 5242880 | bytes 8388768 | tf_op jit(solution)/shard_map/add | solution.py:74
  95.0 4.3 %copy.28 = f32[8,64,1024]{1,0,2:T(8,128)} copy(f32[8,64,1024]{2,0,1:T(8,128)} %multiply_add_fusion) | data formatting | bytes 4194304 | tf_op jit(solution)/shard_map/add | solution.py:74
  99.3 7.2 %reshape.23 = f32[8,1,65536]{2,1,0:T(1,128)} reshape(f32[1024,8,64]{2,1,0:T(8,128)} %bitcast.48) | data formatting | bytes 4194304
  106.5 5.0 %all-to-all-start = ((f32[8,1,65536]{2,1,0:T(1,128)}), f32[8,1,65536]{2,1,0:T(1,128)S(1)}, u32[]{:S(2)}, u32[]{:S(2)}) async-start(f32[8,1,65536]{2,1,0:T(1,128)} %reshape.23), calls=%async_computation | async-start | bytes 4194304 | tf_op jit(solution)/shard_map/all_to_all | solution.py:88
  111.9 2.9 %cholesky.16 = f32[32,32]{1,0:T(8,128)S(1)} custom-call(f32[32,32]{1,0:T(8,128)S(1)} %fusion.26), custom_call_target="Cholesky" | custom-call | tf_op jit(solution)/shard_map/jit(cholesky)/cholesky | solution.py:34
  116.2 2.4 %custom-call.10 = f32[1,32,32]{1,2,0:T(8,128)S(1)} custom-call(f32[1,32,32]{2,1,0:T(8,128)S(1)} %fusion.23), custom_call_target="InvertDiagBlocksLowerTriangular" | custom-call | tf_op jit(solution)/shard_map/jit(_cho_solve)/triangular_solve | solution.py:35
  119.1 41.5 %all-to-all-done = f32[8,1,65536]{2,1,0:T(1,128)S(1)} async-done(((f32[8,1,65536]{2,1,0:T(1,128)}), f32[8,1,65536]{2,1,0:T(1,128)S(1)}, u32[]{:S(2)}, u32[]{:S(2)}) %all-to-all-start) | async-done | bytes 2097184 | tf_op jit(solution)/shard_map/all_to_all | solution.py:88
  160.6 1.3 copy-done.11
  162.4 7.2 %reduce.6 = f32[8,65536]{1,0:T(8,128)S(1)} reduce(f32[8,1,65536]{2,1,0:T(1,128)} %copy-done.11, f32[]{:T(128)} %broadcast.107), dimensions={1}, to_apply=%all_to_all.26.reduce_sub_computation | reduce | bytes 4194308 | tf_op jit(solution)/shard_map/all_to_all | solution.py:88
  169.7 3.6 %reshape.24 = f32[1024,8,64]{2,1,0:T(8,128)} reshape(f32[8,65536]{1,0:T(8,128)S(1)} %reduce.6) | data formatting | bytes 4194304
  173.3 3.8 %copy.29 = f32[8,64,8,128]{3,0,2,1:T(8,128)S(1)} copy(f32[8,64,8,128]{1,0,3,2:T(8,128)} %bitcast.47) | data formatting | bytes 4194304 | tf_op jit(solution)/shard_map/all_to_all | solution.py:88
  178.2 1.6 copy.30
  179.8 3.6 %all-to-all-start.1 = ((f32[32,64,128]{2,1,0:T(8,128)}), f32[32,64,128]{2,1,0:T(8,128)S(1)}, u32[]{:S(2)}, u32[]{:S(2)}) async-start(f32[32,64,128]{2,1,0:T(8,128)} %copy.30), calls=%async_computation.1 | async-start | bytes 2097152 | tf_op jit(solution)/shard_map/all_to_all | solution.py:91
  183.4 2.5 %copy.32 = f32[8,64,1024]{2,1,0:T(8,128)} copy(f32[8,64,1024]{2,0,1:T(8,128)S(1)} %copy-done.10) | data formatting | bytes 4194304
  185.9 23.9 %all-to-all-done.1 = f32[32,64,128]{2,1,0:T(8,128)S(1)} async-done(((f32[32,64,128]{2,1,0:T(8,128)}), f32[32,64,128]{2,1,0:T(8,128)S(1)}, u32[]{:S(2)}, u32[]{:S(2)}) %all-to-all-start.1) | async-done | bytes 1048608 | tf_op jit(solution)/shard_map/all_to_all | solution.py:91
  (72 shorter events, 19.5 us)
Async XLA Ops:
  0.6 3.0 %copy-start.13 = (f32[8,64,1024]{2,1,0:T(8,128)S(1)}, f32[8,64,1024]{2,1,0:T(8,128)}, u32[]{:S(2)}) copy-start(f32[8,64,1024]{2,1,0:T(8,128)} %param.5) | copy-start | bytes 6291460
  4.9 8.3 %collective-permute-start = (f32[2,8,1,1024]{3,1,2,0:T(8,128)S(1)}, f32[2,8,1,1024]{3,1,2,0:T(8,128)S(1)}, u32[]{:S(2)}, u32[]{:S(2)}) collective-permute-start(f32[2,8,1,1024]{3,1,2,0:T(8,128)S(1)} %get-tuple-element.30), channel_id=1, source_target_pairs={{0,1},{1,2},{2,3},{4,5},{5,6},{6,7},{8,9},{9,10},{10,11},{12,13},{... | collective-permute-start | bytes 196616 | tf_op jit(solution)/shard_map/ppermute | solution.py:18
  9.7 2.1 copy-start.12
  9.7 6.3 %collective-permute-start.1 = (f32[2,8,1,1024]{3,1,2,0:T(8,128)S(1)}, f32[2,8,1,1024]{3,1,2,0:T(8,128)S(1)}, u32[]{:S(2)}, u32[]{:S(2)}) collective-permute-start(f32[2,8,1,1024]{3,1,2,0:T(8,128)S(1)} %get-tuple-element.31), channel_id=1, source_target_pairs={{1,0},{2,1},{3,2},{5,4},{6,5},{7,6},{9,8},{10,9},{11,10},{13,12},{... | collective-permute-start | bytes 196616 | tf_op jit(solution)/shard_map/ppermute | solution.py:19
  11.8 13.5 %copy-start.1 = (f32[8,64,1023]{2,0,1:T(8,128)}, f32[8,64,1023]{2,0,1:T(8,128)S(1)}, u32[]{:S(2)}) copy-start(f32[8,64,1023]{2,0,1:T(8,128)S(1)} %slice_multiply_fusion.2) | copy-start | bytes 6285316
  17.2 9.7 %copy-start.5 = (f32[8,65,1024]{2,0,1:T(8,128)}, f32[8,65,1024]{2,0,1:T(8,128)S(1)}, u32[]{:S(2)}) copy-start(f32[8,65,1024]{2,0,1:T(8,128)S(1)} %get-tuple-element.27) | copy-start | bytes 6389764
  18.4 9.1 %copy-start.8 = (f32[8,64,1024]{2,0,1:T(8,128)}, f32[8,64,1024]{2,0,1:T(8,128)S(1)}, u32[]{:S(2)}) copy-start(f32[8,64,1024]{2,0,1:T(8,128)S(1)} %get-tuple-element.25) | copy-start | bytes 6291460
  19.0 6.7 %collective-permute-start.2 = (f32[8,1,1024]{2,0,1:T(8,128)S(1)}, f32[8,1,1024]{2,0,1:T(8,128)S(1)}, u32[]{:S(2)}, u32[]{:S(2)}) collective-permute-start(f32[8,1,1024]{2,0,1:T(8,128)S(1)} %get-tuple-element.37), channel_id=1, source_target_pairs={{1,0},{2,1},{3,2},{5,4},{6,5},{7,6},{9,8},{10,9},{11,10},{13,12},{... | collective-permute-start | bytes 98312 | tf_op jit(solution)/shard_map/ppermute | solution.py:19
  20.3 6.5 %collective-permute-start.3 = (f32[8,1,1024]{2,0,1:T(8,128)S(1)}, f32[8,1,1024]{2,0,1:T(8,128)S(1)}, u32[]{:S(2)}, u32[]{:S(2)}) collective-permute-start(f32[8,1,1024]{2,0,1:T(8,128)S(1)} %get-tuple-element.36), channel_id=1, source_target_pairs={{0,1},{1,2},{2,3},{4,5},{5,6},{6,7},{8,9},{9,10},{10,11},{12,13},{... | collective-permute-start | bytes 98312 | tf_op jit(solution)/shard_map/ppermute | solution.py:18
  43.4 6.8 %copy-start.2 = (f32[8,64,1023]{2,0,1:T(8,128)S(1)}, f32[8,64,1023]{2,0,1:T(8,128)}, u32[]{:S(2)}) copy-start(f32[8,64,1023]{2,0,1:T(8,128)} %copy-done.1) | copy-start | bytes 6285316
  44.1 6.6 %collective-permute-start.4 = (f32[8,1,1024]{2,0,1:T(8,128)S(1)}, f32[8,1,1024]{2,0,1:T(8,128)S(1)}, u32[]{:S(2)}, u32[]{:S(2)}) collective-permute-start(f32[8,1,1024]{2,0,1:T(8,128)S(1)} %get-tuple-element.35), channel_id=1, source_target_pairs={{1,0},{2,1},{3,2},{5,4},{6,5},{7,6},{9,8},{10,9},{11,10},{13,12},{... | collective-permute-start | bytes 98312 | tf_op jit(solution)/shard_map/ppermute | solution.py:19
  45.4 6.3 %copy-start.6 = (f32[8,65,1024]{2,0,1:T(8,128)S(1)}, f32[8,65,1024]{2,0,1:T(8,128)}, u32[]{:S(2)}) copy-start(f32[8,65,1024]{2,0,1:T(8,128)} %copy-done.5) | copy-start | bytes 6389764
  45.4 6.3 %collective-permute-start.5 = (f32[8,1,1024]{2,0,1:T(8,128)S(1)}, f32[8,1,1024]{2,0,1:T(8,128)S(1)}, u32[]{:S(2)}, u32[]{:S(2)}) collective-permute-start(f32[8,1,1024]{2,0,1:T(8,128)S(1)} %get-tuple-element.34), channel_id=1, source_target_pairs={{0,1},{1,2},{2,3},{4,5},{5,6},{6,7},{8,9},{9,10},{10,11},{12,13},{... | collective-permute-start | bytes 98312 | tf_op jit(solution)/shard_map/ppermute | solution.py:18
  50.7 1.4 copy-start.9
  52.1 1.3 copy-start.4
  69.9 8.8 %copy-start = (f32[8,64,1024]{2,0,1:T(8,128)}, f32[8,64,1024]{2,0,1:T(8,128)S(1)}, u32[]{:S(2)}) copy-start(f32[8,64,1024]{2,0,1:T(8,128)S(1)} %multiply_subtract_fusion) | copy-start | bytes 6291460
  69.9 6.8 %copy-start.3 = (f32[8,64,1023]{2,0,1:T(8,128)S(1)}, f32[8,64,1023]{2,0,1:T(8,128)}, u32[]{:S(2)}) copy-start(f32[8,64,1023]{2,0,1:T(8,128)} %copy-done.1) | copy-start | bytes 6285316
  70.6 6.5 %collective-permute-start.6 = (f32[8,1,1024]{2,0,1:T(8,128)S(1)}, f32[8,1,1024]{2,0,1:T(8,128)S(1)}, u32[]{:S(2)}, u32[]{:S(2)}) collective-permute-start(f32[8,1,1024]{2,0,1:T(8,128)S(1)} %get-tuple-element.33), channel_id=1, source_target_pairs={{1,0},{2,1},{3,2},{5,4},{6,5},{7,6},{9,8},{10,9},{11,10},{13,12},{... | collective-permute-start | bytes 98312 | tf_op jit(solution)/shard_map/ppermute | solution.py:19
  72.0 6.3 %copy-start.7 = (f32[8,65,1024]{2,0,1:T(8,128)S(1)}, f32[8,65,1024]{2,0,1:T(8,128)}, u32[]{:S(2)}) copy-start(f32[8,65,1024]{2,0,1:T(8,128)} %copy-done.5) | copy-start | bytes 6389764
  72.0 6.3 %collective-permute-start.7 = (f32[8,1,1024]{2,0,1:T(8,128)S(1)}, f32[8,1,1024]{2,0,1:T(8,128)S(1)}, u32[]{:S(2)}, u32[]{:S(2)}) collective-permute-start(f32[8,1,1024]{2,0,1:T(8,128)S(1)} %get-tuple-element.32), channel_id=1, source_target_pairs={{0,1},{1,2},{2,3},{4,5},{5,6},{6,7},{8,9},{9,10},{10,11},{12,13},{... | collective-permute-start | bytes 98312 | tf_op jit(solution)/shard_map/ppermute | solution.py:18
  106.5 5.0 %copy-start.14 = (s32[64,2]{0,1:T(2,128)S(1)}, s32[64,2]{0,1:T(2,128)}, u32[]{:S(2)}) copy-start(s32[64,2]{0,1:T(2,128)} %param.7) | copy-start | bytes 1540
  106.5 54.0 %all-to-all-start = ((f32[8,1,65536]{2,1,0:T(1,128)}), f32[8,1,65536]{2,1,0:T(1,128)S(1)}, u32[]{:S(2)}, u32[]{:S(2)}) async-start(f32[8,1,65536]{2,1,0:T(1,128)} %reshape.23), calls=%async_computation | async-start | bytes 4194304 | tf_op jit(solution)/shard_map/all_to_all | solution.py:88
  160.6 1.3 copy-start.11
  178.2 5.2 %copy-start.10 = (f32[8,64,1024]{2,0,1:T(8,128)S(1)}, f32[8,64,1024]{2,0,1:T(8,128)}, u32[]{:S(2)}) copy-start(f32[8,64,1024]{2,0,1:T(8,128)} %multiply_add_fusion) | copy-start | bytes 6291460
  179.8 30.1 %all-to-all-start.1 = ((f32[32,64,128]{2,1,0:T(8,128)}), f32[32,64,128]{2,1,0:T(8,128)S(1)}, u32[]{:S(2)}, u32[]{:S(2)}) async-start(f32[32,64,128]{2,1,0:T(8,128)} %copy.30), calls=%async_computation.1 | async-start | bytes 2097152 | tf_op jit(solution)/shard_map/all_to_all | solution.py:91
where the time goes:
time: 212 us; the launch traced here: 211 us
  waiting for transfers between devices  71.6 us (34%)
  other arithmetic  40.3 us (19%)
  starting transfers between devices  33.3 us (16%)
  blocking collectives  32 us (15%)
  local copies, waits for them, and re-layouts  30.8 us (15%)
    all_to_all x1, waiting for transfers between devices, on_device(): lax.all_to_all(solution, 'ifg', split_axis=2, concat_axis=0, tiled=True)  41.5 us
    psum x3, blocking collectives, two_products(): lax.psum((jnp.sum(residual * residual, axis=(1, 2)), jnp.sum(residual * i...  32 us
    all_to_all x1, waiting for transfers between devices, on_device(): lax.all_to_all(local, 'ifg', split_axis=0, concat_axis=2, tiled=True)  23.9 us
    ppermute x4, starting transfers between devices, extended(): before = lax.ppermute(last, axis, up)  19.3 us
    unnamed x35, local copies, waits for them, and re-layouts  19 us
    sub x2, other arithmetic, on_device(): residual = residual - alpha[:, None, None] * along  8.49 us
    all_to_all x1, other arithmetic, on_device(): lax.all_to_all(solution, 'ifg', split_axis=2, concat_axis=0, tiled=True)  7.22 us
    ppermute x4, starting transfers between devices, extended(): after = lax.ppermute(initial, axis, down)  5.43 us
  transfers between devices with their start and end apart: 10, of which 6 were waited for; matrix products, arithmetic and copies ran while one was open for 6% of the time, Pallas kernels for 0%

commit v1 on v0

--- a/solution.py
+++ b/solution.py
@@ -85,7 +85,12 @@
     local = jnp.einsum(
         "dk,krc->drc",
         mapping,
-        lax.all_to_all(solution, "ifg", split_axis=2, concat_axis=0, tiled=True),
+        jnp.concatenate(
+            lax.all_to_all(
+                jnp.stack(jnp.split(solution, lax.axis_size("ifg"), axis=2)), "ifg", 0, 0
+            ),
+            axis=0,
+        ),
         precision=lax.Precision.HIGHEST,
     )
     series = lax.all_to_all(local, "ifg", split_axis=0, concat_axis=2, tiled=True)

time: 212 us -> 187 us (0.88)
  blocking collectives: 32 us -> 61.1 us
  waiting for transfers between devices: 71.6 us -> 48.7 us
  local copies, waits for them, and re-layouts: 30.8 us -> 8.79 us
  other arithmetic: 40.3 us -> 33.9 us
  starting transfers between devices: 33.3 us -> 29.6 us
    all_to_all x0 -> x1, blocking collectives: none -> 29 us  [on_device(): lax.all_to_all(local, 'ifg', split_axis=0, concat_axis=2, tiled=True)]
    all_to_all x2 -> x1, waiting for transfers between devices: 65.5 us -> 41.5 us  [on_device(): lax.all_to_all(jnp.stack(jnp.split(solution, lax.axis_size('ifg'), axis=2...]
    unnamed x35 -> x37, local copies, waits for them, and re-layouts: 19 us -> 5.46 us
    all_to_all x1 -> x0, other arithmetic: 7.22 us -> none  [on_device(): lax.all_to_all(solution, 'ifg', split_axis=2, concat_axis=0, tiled=True)]
    add x1 -> x0, local copies, waits for them, and re-layouts: 4.34 us -> none  [on_device(): solution = solution + alpha[:, None, None] * direction]
    all_to_all x2 -> x0, local copies, waits for them, and re-layouts: 4.32 us -> none  [on_device(): lax.all_to_all(solution, 'ifg', split_axis=2, concat_axis=0, tiled=True)]
    all_to_all x2 -> x1, starting transfers between devices: 8.57 us -> 5.01 us  [on_device(): lax.all_to_all(jnp.stack(jnp.split(solution, lax.axis_size('ifg'), axis=2...]
  transfers between devices with their start and end apart: 10 -> 9, of which waited for: 6 -> 5; matrix products, arithmetic and copies ran while one was open for 6% -> 5% of each run, Pallas kernels for 0% -> 0%
where the time goes in v1:
time: 187 us; the launch traced here: 186 us
  blocking collectives  61.1 us (33%)
  waiting for transfers between devices  48.7 us (26%)
  other arithmetic  33.9 us (18%)
  starting transfers between devices  29.6 us (16%)
  local copies, waits for them, and re-layouts  8.79 us (5%)
  matrix products  3.03 us (2%)
    all_to_all x1, waiting for transfers between devices, on_device(): lax.all_to_all(jnp.stack(jnp.split(solution, lax.axis_size('ifg'), axis=2...  41.5 us
    psum x3, blocking collectives, two_products(): lax.psum((jnp.sum(residual * residual, axis=(1, 2)), jnp.sum(residual * i...  32.2 us
    all_to_all x1, blocking collectives, on_device(): lax.all_to_all(local, 'ifg', split_axis=0, concat_axis=2, tiled=True)  29 us
    ppermute x4, starting transfers between devices, extended(): before = lax.ppermute(last, axis, up)  19.2 us
    sub x2, other arithmetic, on_device(): residual = residual - alpha[:, None, None] * along  8.75 us
    unnamed x37, local copies, waits for them, and re-layouts  5.46 us
    ppermute x4, starting transfers between devices, extended(): after = lax.ppermute(initial, axis, down)  5.43 us
    reduce_sum x3, other arithmetic, two_products(): jnp.sum(residual * image, axis=(1, 2))  5.19 us
  transfers between devices with their start and end apart: 9, of which 5 were waited for; matrix products, arithmetic and copies ran while one was open for 5% of the time, Pallas kernels for 0%

profile of v1, /device:TPU:0, one launch (start us, length us, event | category | flops | bytes accessed | tf_op | source)
XLA Modules:
  0.0 186.3 jit_solution(18030956107212452401)
XLA Ops:
  0.6 1.4 pad_maximum_fusion.2
  2.1 4.9 %collective-permute-start = (f32[2,8,1,1024]{3,2,1,0:T(1,128)S(1)}, f32[2,8,1,1024]{3,2,1,0:T(1,128)S(1)}, u32[]{:S(2)}, u32[]{:S(2)}) collective-permute-start(f32[2,8,1,1024]{3,2,1,0:T(1,128)S(1)} %get-tuple-element.26), channel_id=1, source_target_pairs={{0,1},{1,2},{2,3},{4,5},{5,6},{6,7},{8,9},{9,10},{10,11},{12,13},{... | collective-permute-start | bytes 196616 | tf_op jit(solution)/shard_map/ppermute | solution.py:18
  7.0 1.4 collective-permute-start.1
  9.5 3.8 %collective-permute-done.1 = f32[2,8,1,1024]{3,2,1,0:T(1,128)S(1)} collective-permute-done((f32[2,8,1,1024]{3,2,1,0:T(1,128)S(1)}, f32[2,8,1,1024]{3,2,1,0:T(1,128)S(1)}, u32[]{:S(2)}, u32[]{:S(2)}) %collective-permute-start.1) | collective-permute-done | bytes 65568 | tf_op jit(solution)/shard_map/ppermute | solution.py:19
  14.6 0.8 slice_multiply_fusion
  15.4 1.3 fusion.42
  17.4 1.3 collective-permute-start.2
  18.7 4.9 %collective-permute-start.3 = (f32[8,1,1024]{2,1,0:T(1,128)S(1)}, f32[8,1,1024]{2,1,0:T(1,128)S(1)}, u32[]{:S(2)}, u32[]{:S(2)}) collective-permute-start(f32[8,1,1024]{2,1,0:T(1,128)S(1)} %get-tuple-element.32), channel_id=1, source_target_pairs={{0,1},{1,2},{2,3},{4,5},{5,6},{6,7},{8,9},{9,10},{10,11},{12,13},{... | collective-permute-start | bytes 98312 | tf_op jit(solution)/shard_map/ppermute | solution.py:18
  24.1 1.1 collective-permute-done.3
  26.0 2.6 %multiply_reduce_fusion.3 = (f32[8]{0:T(128)S(1)}, f32[8]{0:T(128)S(1)}, f32[8,64,1024]{2,1,0:T(8,128)}) fusion(f32[8,64,1024]{2,1,0:T(8,128)S(1)} %get-tuple-element.21, f32[8,65,1024]{2,1,0:T(8,128)S(1)} %fusion, f32[8,64,1024]{2,1,0:T(8,128)S(1)} %pad_multiply_fusion.2), kind=kLoop, calls=%fused_computation.46 | loop fusion | flops 5242864 | bytes 10485824 | tf_op jit(solution)/shard_map/reduce_sum | solution.py:49
  28.6 10.7 %all-reduce.10 = (f32[8]{0:T(128)S(1)}, f32[8]{0:T(128)S(1)}) all-reduce(f32[8]{0:T(128)S(1)} %get-tuple-element.7, f32[8]{0:T(128)S(1)} %get-tuple-element.6), channel_id=1, replica_groups=mesh['ifg'=8,'strip'=4] {'strip'}, use_global_device_ids=true, to_apply=%region_1.2 | all-reduce | flops 16 | bytes 128 | tf_op jit(solution)/shard_map/psum | solution.py:48
  39.2 2.7 %multiply_subtract_fusion.1 = f32[8,64,1024]{2,1,0:T(8,128)S(1)} fusion(f32[8,64,1024]{2,1,0:T(8,128)} %get-tuple-element.19, f32[8]{0:T(128)S(1)} %div.29, f32[8,64,1024]{2,1,0:T(8,128)} %copy-done.9), kind=kLoop, calls=%fused_computation.45 | loop fusion | flops 1572864 | bytes 6291488 | tf_op jit(solution)/shard_map/sub | solution.py:75
  42.6 1.3 collective-permute-start.4
  43.9 4.7 %collective-permute-start.5 = (f32[8,1,1024]{2,1,0:T(1,128)S(1)}, f32[8,1,1024]{2,1,0:T(1,128)S(1)}, u32[]{:S(2)}, u32[]{:S(2)}) collective-permute-start(f32[8,1,1024]{2,1,0:T(1,128)S(1)} %get-tuple-element.30), channel_id=1, source_target_pairs={{0,1},{1,2},{2,3},{4,5},{5,6},{6,7},{8,9},{9,10},{10,11},{12,13},{... | collective-permute-start | bytes 98312 | tf_op jit(solution)/shard_map/ppermute | solution.py:18
  49.1 1.1 collective-permute-done.5
  50.8 1.3 multiply_reduce_fusion.1
  52.2 10.8 %all-reduce.9 = (f32[8]{0:T(128)S(1)}, f32[8]{0:T(128)S(1)}) all-reduce(f32[8]{0:T(128)S(1)} %get-tuple-element.5, f32[8]{0:T(128)S(1)} %get-tuple-element.4), channel_id=1, replica_groups=mesh['ifg'=8,'strip'=4] {'strip'}, use_global_device_ids=true, to_apply=%region_5.6 | all-reduce | flops 16 | bytes 128 | tf_op jit(solution)/shard_map/psum | solution.py:48
  63.0 6.0 %multiply_subtract_fusion = f32[8,64,1024]{2,1,0:T(8,128)S(1)} fusion(f32[8,64,1024]{2,1,0:T(8,128)S(1)} %multiply_subtract_fusion.1, f32[8,64,1024]{2,1,0:T(8,128)} %get-tuple-element.19, f32[8]{0:T(128)S(1)} %get-tuple-element.18, f32[8]{0:T(128)S(1)} %get-tuple-element.16, f32[8,65,1024]{2,1,0:T(8,128)} %copy-done.4, f32[8,64,1024]{2,1,0:T(8,128)} %copy-done.10), kind=kLoop, calls=%fused_computation.41 | loop fusion | flops 4718592 | bytes 12582976 | tf_op jit(solution)/shard_map/sub | solution.py:75
  69.8 1.4 collective-permute-start.6
  71.2 4.7 %collective-permute-start.7 = (f32[8,1,1024]{2,1,0:T(1,128)S(1)}, f32[8,1,1024]{2,1,0:T(1,128)S(1)}, u32[]{:S(2)}, u32[]{:S(2)}) collective-permute-start(f32[8,1,1024]{2,1,0:T(1,128)S(1)} %get-tuple-element.28), channel_id=1, source_target_pairs={{0,1},{1,2},{2,3},{4,5},{5,6},{6,7},{8,9},{9,10},{10,11},{12,13},{... | collective-permute-start | bytes 98312 | tf_op jit(solution)/shard_map/ppermute | solution.py:18
  76.3 1.2 collective-permute-done.7
  78.1 1.3 fusion.19
  79.4 10.7 %all-reduce.8 = (f32[8]{0:T(128)S(1)}, f32[8]{0:T(128)S(1)}) all-reduce(f32[8]{0:T(128)S(1)} %get-tuple-element.3, f32[8]{0:T(128)S(1)} %get-tuple-element.2), channel_id=1, replica_groups=mesh['ifg'=8,'strip'=4] {'strip'}, use_global_device_ids=true, to_apply=%region_9.10 | all-reduce | flops 16 | bytes 128 | tf_op jit(solution)/shard_map/psum | solution.py:48
  90.1 3.1 %multiply_add_fusion = f32[8,64,1024]{2,1,0:T(8,128)S(1)} fusion(f32[8,64,1024]{2,1,0:T(8,128)} %copy-done, f32[8,64,1024]{2,1,0:T(8,128)S(1)} %multiply_subtract_fusion.1, f32[8]{0:T(128)S(1)} %get-tuple-element.15, f32[8]{0:T(128)S(1)} %get-tuple-element.14, f32[8]{0:T(128)S(1)} %get-tuple-element.18, f32[8]{0:T(128)S(1)} %get-tuple-element.16, ...), kind=kLoop, calls=%fused_computation.38 | loop fusion | flops 5242880 | bytes 8388768 | tf_op jit(solution)/shard_map/add | solution.py:74
  93.2 0.8 fusion.30
  99.2 5.0 %all-to-all-start = ((f32[8,8,64,128]{3,2,1,0:T(8,128)}), f32[8,8,64,128]{3,2,1,0:T(8,128)S(1)}, u32[]{:S(2)}, u32[]{:S(2)}) async-start(f32[8,8,64,128]{3,2,1,0:T(8,128)} %fusion.23), calls=%async_computation | async-start | bytes 4194304 | tf_op jit(solution)/shard_map/all_to_all | solution.py:89
  104.6 2.9 %cholesky.16 = f32[32,32]{1,0:T(8,128)S(1)} custom-call(f32[32,32]{1,0:T(8,128)S(1)} %fusion.35), custom_call_target="Cholesky" | custom-call | tf_op jit(solution)/shard_map/jit(cholesky)/cholesky | solution.py:34
  108.9 2.4 %custom-call.10 = f32[1,32,32]{1,2,0:T(8,128)S(1)} custom-call(f32[1,32,32]{2,1,0:T(8,128)S(1)} %fusion.32), custom_call_target="InvertDiagBlocksLowerTriangular" | custom-call | tf_op jit(solution)/shard_map/jit(_cho_solve)/triangular_solve | solution.py:35
  111.7 41.5 %all-to-all-done = f32[8,8,64,128]{3,2,1,0:T(8,128)S(1)} async-done(((f32[8,8,64,128]{3,2,1,0:T(8,128)}), f32[8,8,64,128]{3,2,1,0:T(8,128)S(1)}, u32[]{:S(2)}, u32[]{:S(2)}) %all-to-all-start) | async-done | bytes 2097184 | tf_op jit(solution)/shard_map/all_to_all | solution.py:89
  153.3 2.3 %fusion.20 = f32[32,64,128]{2,0,1:T(8,128)S(1)} fusion(f32[32,64,1]{1,0,2:T(8,128)S(1)} %convolution_bitcast_fusion, f32[8,8,64,128]{3,2,1,0:T(8,128)S(1)} %all-to-all-done), kind=kOutput, calls=%fused_computation.35 | convolution fusion | flops 201326592 | bytes 3153920 | tf_op jit(solution)/shard_map/dk,krc->drc/dot_general | solution.py:85
  156.2 29.0 %all_to_all.23 = f32[32,64,128]{2,1,0:T(8,128)S(1)} all-to-all(f32[32,64,128]{2,1,0:T(8,128)S(1)} %copy.13), channel_id=1, replica_groups=mesh['ifg'=8,'strip'=4] {'ifg'}, dimensions={0} | all-to-all | bytes 2097152 | tf_op jit(solution)/shard_map/all_to_all | solution.py:96
  185.2 1.1 copy.22
  (70 shorter events, 15.6 us)
Async XLA Ops:
  0.6 7.8 %copy-start.8 = (f32[8,64,1024]{2,1,0:T(8,128)S(1)}, f32[8,64,1024]{2,1,0:T(8,128)}, u32[]{:S(2)}) copy-start(f32[8,64,1024]{2,1,0:T(8,128)} %param.6) | copy-start | bytes 6291460
  2.1 7.4 %collective-permute-start = (f32[2,8,1,1024]{3,2,1,0:T(1,128)S(1)}, f32[2,8,1,1024]{3,2,1,0:T(1,128)S(1)}, u32[]{:S(2)}, u32[]{:S(2)}) collective-permute-start(f32[2,8,1,1024]{3,2,1,0:T(1,128)S(1)} %get-tuple-element.26), channel_id=1, source_target_pairs={{0,1},{1,2},{2,3},{4,5},{5,6},{6,7},{8,9},{9,10},{10,11},{12,13},{... | collective-permute-start | bytes 196616 | tf_op jit(solution)/shard_map/ppermute | solution.py:18
  7.0 2.1 %copy-start.13 = (f32[8,64,1024]{2,1,0:T(8,128)S(1)}, f32[8,64,1024]{2,1,0:T(8,128)}, u32[]{:S(2)}) copy-start(f32[8,64,1024]{2,1,0:T(8,128)} %param.4) | copy-start | bytes 6291460
  7.0 6.3 %collective-permute-start.1 = (f32[2,8,1,1024]{3,2,1,0:T(1,128)S(1)}, f32[2,8,1,1024]{3,2,1,0:T(1,128)S(1)}, u32[]{:S(2)}, u32[]{:S(2)}) collective-permute-start(f32[2,8,1,1024]{3,2,1,0:T(1,128)S(1)} %get-tuple-element.27), channel_id=1, source_target_pairs={{1,0},{2,1},{3,2},{5,4},{6,5},{7,6},{9,8},{10,9},{11,10},{13,12},{... | collective-permute-start | bytes 196616 | tf_op jit(solution)/shard_map/ppermute | solution.py:19
  9.0 14.6 %copy-start.1 = (f32[8,64,1023]{2,1,0:T(8,128)}, f32[8,64,1023]{2,1,0:T(8,128)S(1)}, u32[]{:S(2)}) copy-start(f32[8,64,1023]{2,1,0:T(8,128)S(1)} %slice_multiply_fusion.2) | copy-start | bytes 6285316
  9.0 4.2 %copy-start.12 = (f32[8,64,1024]{2,1,0:T(8,128)S(1)}, f32[8,64,1024]{2,1,0:T(8,128)}, u32[]{:S(2)}) copy-start(f32[8,64,1024]{2,1,0:T(8,128)} %param.5) | copy-start | bytes 6291460
  15.4 9.8 %copy-start.5 = (f32[8,65,1024]{2,1,0:T(8,128)}, f32[8,65,1024]{2,1,0:T(8,128)S(1)}, u32[]{:S(2)}) copy-start(f32[8,65,1024]{2,1,0:T(8,128)S(1)} %get-tuple-element.23) | copy-start | bytes 6389764
  16.7 9.3 %copy-start.9 = (f32[8,64,1024]{2,1,0:T(8,128)}, f32[8,64,1024]{2,1,0:T(8,128)S(1)}, u32[]{:S(2)}) copy-start(f32[8,64,1024]{2,1,0:T(8,128)S(1)} %get-tuple-element.21) | copy-start | bytes 6291460
  17.4 6.7 %collective-permute-start.2 = (f32[8,1,1024]{2,1,0:T(1,128)S(1)}, f32[8,1,1024]{2,1,0:T(1,128)S(1)}, u32[]{:S(2)}, u32[]{:S(2)}) collective-permute-start(f32[8,1,1024]{2,1,0:T(1,128)S(1)} %get-tuple-element.33), channel_id=1, source_target_pairs={{1,0},{2,1},{3,2},{5,4},{6,5},{7,6},{9,8},{10,9},{11,10},{13,12},{... | collective-permute-start | bytes 98312 | tf_op jit(solution)/shard_map/ppermute | solution.py:19
  18.7 6.5 %collective-permute-start.3 = (f32[8,1,1024]{2,1,0:T(1,128)S(1)}, f32[8,1,1024]{2,1,0:T(1,128)S(1)}, u32[]{:S(2)}, u32[]{:S(2)}) collective-permute-start(f32[8,1,1024]{2,1,0:T(1,128)S(1)} %get-tuple-element.32), channel_id=1, source_target_pairs={{0,1},{1,2},{2,3},{4,5},{5,6},{6,7},{8,9},{9,10},{10,11},{12,13},{... | collective-permute-start | bytes 98312 | tf_op jit(solution)/shard_map/ppermute | solution.py:18
  41.9 6.7 %copy-start.2 = (f32[8,64,1023]{2,1,0:T(8,128)S(1)}, f32[8,64,1023]{2,1,0:T(8,128)}, u32[]{:S(2)}) copy-start(f32[8,64,1023]{2,1,0:T(8,128)} %copy-done.1) | copy-start | bytes 6285316
  42.6 6.4 %collective-permute-start.4 = (f32[8,1,1024]{2,1,0:T(1,128)S(1)}, f32[8,1,1024]{2,1,0:T(1,128)S(1)}, u32[]{:S(2)}, u32[]{:S(2)}) collective-permute-start(f32[8,1,1024]{2,1,0:T(1,128)S(1)} %get-tuple-element.31), channel_id=1, source_target_pairs={{1,0},{2,1},{3,2},{5,4},{6,5},{7,6},{9,8},{10,9},{11,10},{13,12},{... | collective-permute-start | bytes 98312 | tf_op jit(solution)/shard_map/ppermute | solution.py:19
  43.9 6.3 %copy-start.6 = (f32[8,65,1024]{2,1,0:T(8,128)S(1)}, f32[8,65,1024]{2,1,0:T(8,128)}, u32[]{:S(2)}) copy-start(f32[8,65,1024]{2,1,0:T(8,128)} %copy-done.5) | copy-start | bytes 6389764
  43.9 6.3 %collective-permute-start.5 = (f32[8,1,1024]{2,1,0:T(1,128)S(1)}, f32[8,1,1024]{2,1,0:T(1,128)S(1)}, u32[]{:S(2)}, u32[]{:S(2)}) collective-permute-start(f32[8,1,1024]{2,1,0:T(1,128)S(1)} %get-tuple-element.30), channel_id=1, source_target_pairs={{0,1},{1,2},{2,3},{4,5},{5,6},{6,7},{8,9},{9,10},{10,11},{12,13},{... | collective-permute-start | bytes 98312 | tf_op jit(solution)/shard_map/ppermute | solution.py:18
  49.0 1.7 copy-start.10
  50.8 1.4 copy-start.4
  69.1 9.0 %copy-start = (f32[8,64,1024]{2,1,0:T(8,128)}, f32[8,64,1024]{2,1,0:T(8,128)S(1)}, u32[]{:S(2)}) copy-start(f32[8,64,1024]{2,1,0:T(8,128)S(1)} %multiply_subtract_fusion) | copy-start | bytes 6291460
  69.1 6.8 %copy-start.3 = (f32[8,64,1023]{2,1,0:T(8,128)S(1)}, f32[8,64,1023]{2,1,0:T(8,128)}, u32[]{:S(2)}) copy-start(f32[8,64,1023]{2,1,0:T(8,128)} %copy-done.1) | copy-start | bytes 6285316
  69.8 6.5 %collective-permute-start.6 = (f32[8,1,1024]{2,1,0:T(1,128)S(1)}, f32[8,1,1024]{2,1,0:T(1,128)S(1)}, u32[]{:S(2)}, u32[]{:S(2)}) collective-permute-start(f32[8,1,1024]{2,1,0:T(1,128)S(1)} %get-tuple-element.29), channel_id=1, source_target_pairs={{1,0},{2,1},{3,2},{5,4},{6,5},{7,6},{9,8},{10,9},{11,10},{13,12},{... | collective-permute-start | bytes 98312 | tf_op jit(solution)/shard_map/ppermute | solution.py:19
  71.2 6.3 %copy-start.7 = (f32[8,65,1024]{2,1,0:T(8,128)S(1)}, f32[8,65,1024]{2,1,0:T(8,128)}, u32[]{:S(2)}) copy-start(f32[8,65,1024]{2,1,0:T(8,128)} %copy-done.5) | copy-start | bytes 6389764
  71.2 6.3 %collective-permute-start.7 = (f32[8,1,1024]{2,1,0:T(1,128)S(1)}, f32[8,1,1024]{2,1,0:T(1,128)S(1)}, u32[]{:S(2)}, u32[]{:S(2)}) collective-permute-start(f32[8,1,1024]{2,1,0:T(1,128)S(1)} %get-tuple-element.28), channel_id=1, source_target_pairs={{0,1},{1,2},{2,3},{4,5},{5,6},{6,7},{8,9},{9,10},{10,11},{12,13},{... | collective-permute-start | bytes 98312 | tf_op jit(solution)/shard_map/ppermute | solution.py:18
  93.2 5.3 %copy-start.11 = (f32[8,64,1024]{2,1,0:T(8,128)}, f32[8,64,1024]{2,1,0:T(8,128)S(1)}, u32[]{:S(2)}) copy-start(f32[8,64,1024]{2,1,0:T(8,128)S(1)} %multiply_add_fusion) | copy-start | bytes 6291460
  99.2 5.0 %copy-start.14 = (s32[64,2]{0,1:T(2,128)S(1)}, s32[64,2]{0,1:T(2,128)}, u32[]{:S(2)}) copy-start(s32[64,2]{0,1:T(2,128)} %param.7) | copy-start | bytes 1540
  99.2 54.0 %all-to-all-start = ((f32[8,8,64,128]{3,2,1,0:T(8,128)}), f32[8,8,64,128]{3,2,1,0:T(8,128)S(1)}, u32[]{:S(2)}, u32[]{:S(2)}) async-start(f32[8,8,64,128]{3,2,1,0:T(8,128)} %fusion.23), calls=%async_computation | async-start | bytes 4194304 | tf_op jit(solution)/shard_map/all_to_all | solution.py:89
